TPU v7x, 32 devices: a whole 2x2x4 slice. The times are simulated.
32 devices in a mesh: fsdp: 4 (over z), ctx: 8 (over y, x, core).
Axes of the slice: x: 2, y: 2, z: 4, core: 2. Of those that a mesh axis runs over, the one named last changes fastest.
Arguments:
- query: bfloat16 [4, 2048, 4096], P('fsdp', 'ctx'), may hold values from -2.5 to 2.5
- key_value_rows: bfloat16 [4, 2048, 1024], P('fsdp', 'ctx'), may hold values from -2.5 to 2.5
- grad_out: bfloat16 [4, 2048, 4096], P('fsdp', 'ctx'), may hold values from -6 to 6
- doc_lengths: int32 [4, 8], P('fsdp'), may hold values from 1 to 512, 2048 in all within a row
- key_value_weight: bfloat16 [4096, 1024], P(('fsdp', 'ctx')), may hold values from -0.1875 to 0.1875
Outputs:
- grad_query: bfloat16 [4, 2048, 4096], P('fsdp', 'ctx')
- grad_kv: bfloat16 [4, 2048, 1024], P('fsdp', 'ctx')
- grad_input: bfloat16 [4, 2048, 4096], P('fsdp', 'ctx')
Inputs may be any that keep to these rules, and one draw needn't show every extreme that they name: `doc_lengths`: each row sums to 2048; in each row the longest document has exactly 512 tokens.
All inputs are finite; a program needn't handle non-finite values.
Results may differ from a plain program's by a relative error of at most 0.0059.
Values may be sent and summed in bfloat16 or wider, within the bound.
A program may use at most 128 MiB of HBM per device.

v0:
```python
import functools

import jax
import jax.numpy as jnp
from jax import lax
from jax.experimental import pallas as pl
from jax.experimental.pallas import tpu as pltpu
from jax.sharding import PartitionSpec as P

QUERY_HEAD_COUNT = 32
KEY_VALUE_HEADS = 4
HEAD_SIZE = 128
DOC_SHARDS = 2
GROUP = QUERY_HEAD_COUNT // KEY_VALUE_HEADS
LOG2E = 1.4426950408889634


def dot(a, b, dims):
    return lax.dot_general(a, b, (dims, ((), ())), preferred_element_type=jnp.float32)


def gradients_kernel(
    shape, lengths, query_hbm, grad_hbm, kv_hbm, w_own, grad_query, grad_kv, w_all,
    query, grad, kv0, in_sem, kv_sem,
    window, staged, landed, own, bias, dk, dv,
    kv_send, kv_recv, g_send, g_recv, z_send, r_send, l_send, p_send, w_recv, p_recv, local_sem,
):
    shards, count = shape
    chips = count // 2
    half = chips // 2
    width = int(chips ** 0.5)
    rows = query.shape[0]
    group_width = GROUP * HEAD_SIZE
    w_rows = w_own.shape[0]
    keys = (DOC_SHARDS + 1) * rows
    scale = HEAD_SIZE ** (-0.5)
    z = lax.axis_index("fsdp")
    me = lax.axis_index("ctx")
    core = lax.rem(me, 2)
    chip = me // 2
    line = chip // width
    column = lax.rem(chip, width)
    odd = lax.rem(line, 2)
    place = line * width + column + odd * (width - 1 - 2 * column)

    def ring_ctx(spot):
        spot = lax.rem(spot + chips, chips)
        row = spot // width
        col = lax.rem(spot, width)
        return 2 * (row * width + col + lax.rem(row, 2) * (width - 1 - 2 * col)) + core

    right = ring_ctx(place + 1)
    left = ring_ctx(place - 1)
    partner = me + 1 - 2 * core

    def query_in(g):
        cols = pl.ds(pl.multiple_of(g * group_width, HEAD_SIZE), group_width)
        return pltpu.make_async_copy(query_hbm.at[:, cols], query.at[:, cols], in_sem.at[0, g])

    def grad_in(g):
        cols = pl.ds(pl.multiple_of(g * group_width, HEAD_SIZE), group_width)
        return pltpu.make_async_copy(grad_hbm.at[:, cols], grad.at[:, cols], in_sem.at[1, g])

    kv_in = pltpu.make_async_copy(kv_hbm, kv0, kv_sem)
    kv_in.start()
    for g in range(KEY_VALUE_HEADS):
        query_in(g).start()
        grad_in(g).start()

    barrier = pltpu.get_barrier_semaphore()
    peers = [(z, lax.rem(me + o + count, count)) for o in (1, 2, -1, -2)]
    peers += [(lax.rem(z + r, shards), me) for r in range(1, shards)]
    peers += [(z, right), (z, left), (z, partner)]
    for peer in peers:
        pl.semaphore_signal(barrier, inc=1, device_id=peer, device_id_type=pl.DeviceIdType.MESH)
    pl.semaphore_wait(barrier, len(peers))

    def remote(src, dst, send, recv, device):
        return pltpu.make_async_remote_copy(
            src_ref=src, dst_ref=dst, send_sem=send, recv_sem=recv,
            device_id=device, device_id_type=pl.DeviceIdType.MESH,
        )

    def kv_copy(o, g, part):
        cols = pl.ds(pl.multiple_of((part * KEY_VALUE_HEADS + g) * HEAD_SIZE, HEAD_SIZE), HEAD_SIZE)
        return remote(
            kv_hbm.at[:, cols], window.at[o, :, cols], kv_send.at[o, g, part], kv_recv.at[o, g, part],
            (z, lax.rem(me + o + 1, count)),
        )

    def kv_relay(g, part):
        cols = pl.ds(pl.multiple_of((part * KEY_VALUE_HEADS + g) * HEAD_SIZE, HEAD_SIZE), HEAD_SIZE)
        return remote(
            window.at[1, :, cols], window.at[0, :, cols], kv_send.at[0, g, part], kv_recv.at[0, g, part],
            (z, partner),
        )

    sends_kv = [core == 0, me + 2 < count]
    relays_kv = (core == 1) & (me >= 2)

    def grad_copy(o, g):
        return remote(
            staged.at[o, g], landed.at[o, g], g_send.at[o, g], g_recv.at[o, g],
            (z, lax.rem(me - o - 1 + count, count)),
        )

    def block(zz, spot, flip=False):
        at = ring_ctx(spot)
        if flip:
            at = at + 1 - 2 * core
        return w_all.at[pl.ds(pl.multiple_of((zz * count + at) * w_rows, w_rows), w_rows)]

    def w_copy(zz, spot, sems, arrive, device, mine=False):
        spot = lax.rem(spot + chips, chips)
        src = w_own if mine else block(zz, spot)
        return remote(src, block(zz, spot), sems.at[zz, spot], arrive.at[zz, spot], device)

    def shard(r):
        return lax.rem(z - r + shards, shards)

    def w_arrived(r, t):
        w_copy(shard(r), place + t, r_send, w_recv, (z, right)).wait_recv()

    def takes_right(spot, zz):
        at = lax.rem(lax.rem(spot + chips, chips), 4)
        turn = lax.rem(zz, 4)
        even = lax.rem(at, 2) == 0
        return even | ((at == 1) & (turn >= 1)) | ((at == 3) & (turn >= 2))

    def each_copy(r, t, act):
        zz = shard(r)
        mine = r == 0 and t == 0
        if t == 0:
            act(w_copy(zz, place, r_send, w_recv, (z, right), mine))
            act(w_copy(zz, place, l_send, w_recv, (z, left), mine))
        elif -half + 1 <= t < 0:
            copy = w_copy(zz, place + t, r_send, w_recv, (z, right))
            if t > -half + 1:
                act(copy)
            else:
                pl.when(takes_right(place + 1, zz))(lambda: act(copy))
        elif 0 < t <= half - 1:
            copy = w_copy(zz, place + t, l_send, w_recv, (z, left))
            if t < half - 1:
                act(copy)
            else:
                pl.when(jnp.logical_not(takes_right(place - 1, zz)))(lambda: act(copy))
        act(w_copy(zz, place + t, p_send, p_recv, (z, partner), mine))

    def z_copy(r):
        to = lax.rem(z + r, shards)
        return remote(w_own, block(z, place), z_send.at[to], w_recv.at[z, place], (to, me))

    for g in range(KEY_VALUE_HEADS):
        for o in range(DOC_SHARDS):
            @pl.when(sends_kv[o])
            def _():
                kv_copy(o, g, 0).start()
                kv_copy(o, g, 1).start()

    for r in range(1, shards):
        z_copy(r).start()
    each_copy(0, 0, lambda c: c.start())
    local = pltpu.make_async_copy(w_own, block(z, place), local_sem)
    local.start()

    for o in range(DOC_SHARDS):
        @pl.when(me < o + 1)
        def _():
            window[o] = jnp.zeros(window.shape[1:], window.dtype)

        @pl.when(me + o + 1 >= count)
        def _():
            landed[o] = jnp.zeros(landed.shape[1:], landed.dtype)

    first = me * rows
    pos = first + lax.broadcasted_iota(jnp.int32, (1, rows), 1)
    start = jnp.zeros((1, rows), jnp.int32)
    end = jnp.int32(0)
    for d in range(lengths.shape[1]):
        end = end + lengths[0, d]
        start = jnp.where(pos >= end, end, start)
    key_pos = first - DOC_SHARDS * rows + lax.broadcasted_iota(jnp.int32, (keys, rows), 0)
    live = (key_pos >= start) & (key_pos <= pos)
    bias[...] = jnp.where(live, 0.0, -1e30)

    def group(g, carry):
        for o in reversed(range(DOC_SHARDS)):
            @pl.when(me >= o + 1)
            def _():
                kv_copy(o, g, 0).wait_recv()
                kv_copy(o, g, 1).wait_recv()

            if o == 1:
                @pl.when(relays_kv)
                def _():
                    kv_relay(g, 0).start()
                    kv_relay(g, 1).start()
        query_in(g).wait()
        grad_in(g).wait()

        @pl.when(g == 0)
        def _():
            kv_in.wait()
        kc = pl.ds(pl.multiple_of(g * HEAD_SIZE, HEAD_SIZE), HEAD_SIZE)
        vc = pl.ds(pl.multiple_of((g + KEY_VALUE_HEADS) * HEAD_SIZE, HEAD_SIZE), HEAD_SIZE)
        key = jnp.concatenate([window[1, :, kc], window[0, :, kc], kv0[:, kc]], axis=0)
        value = jnp.concatenate([window[1, :, vc], window[0, :, vc], kv0[:, vc]], axis=0)
        dk[...] = jnp.zeros_like(dk)
        dv[...] = jnp.zeros_like(dv)
        for h in range(GROUP):
            cols = pl.ds(pl.multiple_of((g * GROUP + h) * HEAD_SIZE, HEAD_SIZE), HEAD_SIZE)
            q = query[:, cols]
            go = grad[:, cols]
            s = dot(key, q, ((1,), (1,)))
            e = jnp.exp2(s * (scale * LOG2E) + bias[...])
            dp = dot(value, go, ((1,), (1,)))
            inv = 1.0 / jnp.sum(e, axis=0, keepdims=True)
            delta = jnp.sum(e * dp, axis=0, keepdims=True) * inv
            p = e * inv
            ds = (p * (dp - delta)).astype(jnp.bfloat16)
            dv[...] += dot(p.astype(jnp.bfloat16), go, ((1,), (0,)))
            dk[...] += dot(ds, q, ((1,), (0,)))
            dq = dot(key, ds, ((0,), (0,)))
            grad_query[:, cols] = (dq * scale).T.astype(jnp.bfloat16)
        for o in range(DOC_SHARDS):
            part = slice((DOC_SHARDS - 1 - o) * rows, (DOC_SHARDS - o) * rows)
            staged[o, g, 0] = (dk[part, :] * scale).astype(jnp.bfloat16)
            staged[o, g, 1] = dv[part, :].astype(jnp.bfloat16)
        own[g, 0] = dk[DOC_SHARDS * rows:, :] * scale
        own[g, 1] = dv[DOC_SHARDS * rows:, :]
        for o in range(DOC_SHARDS):
            @pl.when(me >= o + 1)
            def _():
                grad_copy(o, g).start()
        for k in range(KEY_VALUE_HEADS):
            turn = [r for r in range(1, shards) if min(r - 1, KEY_VALUE_HEADS - 1) == k]
            if turn:
                @pl.when(g == k)
                def _():
                    for r in turn:
                        w_arrived(r, 0)
                        each_copy(r, 0, lambda c: c.start())
        return carry

    lax.fori_loop(0, KEY_VALUE_HEADS, group, 0)

    for t in range(1, half):
        for r in range(shards):
            for side in (-t, t):
                w_arrived(r, side)
                each_copy(r, side, lambda c: c.start())

    for g in range(KEY_VALUE_HEADS):
        for o in range(DOC_SHARDS):
            @pl.when(me + o + 1 < count)
            def _():
                grad_copy(o, g).wait_recv()
        for part in range(2):
            total = own[g, part]
            for o in range(DOC_SHARDS):
                total = total + landed[o, g, part].astype(jnp.float32)
            at = (part * KEY_VALUE_HEADS + g) * HEAD_SIZE
            grad_kv[:, at:at + HEAD_SIZE] = total.astype(jnp.bfloat16)

    for r in range(shards):
        w_arrived(r, half)
        each_copy(r, half, lambda c: c.start())

    for r in range(shards):
        for t in range(-half + 1, half + 1):
            w_copy(shard(r), place + t, p_send, p_recv, (z, partner)).wait_recv()
            each_copy(r, t, lambda c: c.wait_send())
    for r in range(1, shards):
        z_copy(r).wait_send()
    local.wait()
    for g in range(KEY_VALUE_HEADS):
        @pl.when(relays_kv)
        def _():
            kv_relay(g, 0).wait_send()
            kv_relay(g, 1).wait_send()

        for o in range(DOC_SHARDS):
            @pl.when(sends_kv[o])
            def _():
                kv_copy(o, g, 0).wait_send()
                kv_copy(o, g, 1).wait_send()

            @pl.when(me >= o + 1)
            def _():
                grad_copy(o, g).wait_send()


def gradients(shape, lengths, query, grad, kv0, w_own):
    rows, width = query.shape
    keys = (DOC_SHARDS + 1) * rows
    w_rows, columns = w_own.shape
    shards, count = shape
    chips = count // 2
    vmem = pl.BlockSpec(memory_space=pltpu.VMEM)
    dma = pltpu.SemaphoreType.DMA
    parts = (DOC_SHARDS, KEY_VALUE_HEADS, 2, rows, HEAD_SIZE)
    return pl.pallas_call(
        functools.partial(gradients_kernel, shape),
        in_specs=[pl.BlockSpec(memory_space=pltpu.SMEM)] + [pl.BlockSpec(memory_space=pltpu.HBM)] * 4,
        out_specs=[vmem, vmem, pl.BlockSpec(memory_space=pl.ANY)],
        out_shape=[
            jax.ShapeDtypeStruct((rows, width), jnp.bfloat16),
            jax.ShapeDtypeStruct((rows, columns), jnp.bfloat16),
            jax.ShapeDtypeStruct((w_rows * shards * count, columns), jnp.bfloat16),
        ],
        scratch_shapes=[
            pltpu.VMEM((rows, width), jnp.bfloat16),
            pltpu.VMEM((rows, width), jnp.bfloat16),
            pltpu.VMEM((rows, columns), jnp.bfloat16),
            dma((2, KEY_VALUE_HEADS)),
            dma,
            pltpu.VMEM((DOC_SHARDS, rows, columns), jnp.bfloat16),
            pltpu.VMEM(parts, jnp.bfloat16),
            pltpu.VMEM(parts, jnp.bfloat16),
            pltpu.VMEM(parts[1:], jnp.float32),
            pltpu.VMEM((keys, rows), jnp.float32),
            pltpu.VMEM((keys, HEAD_SIZE), jnp.float32),
            pltpu.VMEM((keys, HEAD_SIZE), jnp.float32),
            dma((DOC_SHARDS, KEY_VALUE_HEADS, 2)),
            dma((DOC_SHARDS, KEY_VALUE_HEADS, 2)),
            dma((DOC_SHARDS, KEY_VALUE_HEADS)),
            dma((DOC_SHARDS, KEY_VALUE_HEADS)),
            dma((shards,)),
            dma((shards, chips)),
            dma((shards, chips)),
            dma((shards, chips)),
            dma((shards, chips)),
            dma((shards, chips)),
            dma,
        ],
        compiler_params=pltpu.CompilerParams(
            vmem_limit_bytes=67043328, collective_id=0, has_side_effects=True
        ),
    )(lengths, query, grad, kv0, w_own)


def body(query, key_value_rows, grad_out, doc_lengths, key_value_weight):
    shape = (lax.axis_size("fsdp"), lax.axis_size("ctx"))
    grad_query, grad_kv, weight = gradients(
        shape, doc_lengths, query[0], grad_out[0], key_value_rows[0], key_value_weight
    )
    grad_input = jnp.einsum("rc,dc->rd", grad_kv, weight, preferred_element_type=jnp.float32)
    return (grad_query[None], grad_kv[None], grad_input.astype(jnp.bfloat16)[None])


def solution(mesh):
    in_specs = (
        P("fsdp", "ctx", None),
        P("fsdp", "ctx", None),
        P("fsdp", "ctx", None),
        P("fsdp", None),
        P(("fsdp", "ctx"), None),
    )
    out_specs = (P("fsdp", "ctx", None), P("fsdp", "ctx", None), P("fsdp", "ctx", None))
    return jax.shard_map(body, mesh=mesh, in_specs=in_specs, out_specs=out_specs, check_vma=False)
```

profile of v0, /device:TPU:25, one launch (start us, length us, event | category | flops | bytes accessed | tf_op | source)
XLA Modules:
  0.0 77.9 jit_solution(5903524464022945588)
XLA Ops:
  0.6 67.7 %shard_map.76 = (bf16[256,4096]{1,0:T(8,128)(2,1)}, bf16[256,1024]{1,0:T(8,128)(2,1)}, bf16[4096,1024]{1,0:T(8,128)(2,1)}) custom-call(s32[1,8]{1,0:T(1,128)} %lengths.1, bf16[256,4096]{1,0:T(8,128)(2,1)} %bitcast.9, bf16[256,4096]{1,0:T(8,128)(2,1)} %bitcast.10, bf16[256,1024]{1,0:T(8,128)(2,1)} %bitcast.12, bf16[128,1024]{1,0:T(8,128)(2,1)} %w_own.1), custom_call_target="tpu_custom_call" | custom-call | tf_op jit(solution)/shard_map/pallas_call | solution.py:303
  68.3 0.0 copy-start
  68.3 7.4 %fusion = bf16[1,256,4096]{2,1,0:T(8,128)(2,1)} fusion(bf16[256,1024]{1,0:T(8,128)(2,1)} %get-tuple-element.7, bf16[4096,1024]{1,0:T(8,128)(2,1)} %get-tuple-element.8), kind=kOutput, calls=%fused_computation.1 | convolution fusion | flops 2148532224 | bytes 11010048 | tf_op jit(solution)/shard_map/rc,dc->rd/dot_general | solution.py:348
  75.7 0.0 copy-done
  75.7 0.0 copy-start.1
  75.7 1.3 %copy.10 = bf16[1,256,4096]{2,1,0:T(8,128)(2,1)} copy(bf16[1,256,4096]{2,1,0:T(8,128)(2,1)S(1)} %bitcast.11) | data formatting | bytes 4194304
  77.0 0.1 copy-done.1
  77.1 0.8 %copy.11 = bf16[1,256,1024]{2,1,0:T(8,128)(2,1)} copy(bf16[1,256,1024]{2,1,0:T(8,128)(2,1)S(1)} %bitcast.13) | data formatting | bytes 1048576
Async XLA Ops:
  68.3 7.4 %copy-start = (bf16[256,4096]{1,0:T(8,128)(2,1)S(1)}, bf16[256,4096]{1,0:T(8,128)(2,1)}, u32[]{:S(2)}) copy-start(bf16[256,4096]{1,0:T(8,128)(2,1)} %get-tuple-element.6) | copy-start | bytes 6291460
  75.7 1.4 %copy-start.1 = (bf16[256,1024]{1,0:T(8,128)(2,1)S(1)}, bf16[256,1024]{1,0:T(8,128)(2,1)}, u32[]{:S(2)}) copy-start(bf16[256,1024]{1,0:T(8,128)(2,1)} %get-tuple-element.7) | copy-start | bytes 1572868
where the time goes:
time: 78.1 us; the launch traced here: 77.9 us
  Pallas kernels  67.7 us (87%)
  matrix products  7.38 us (9%)
  local copies, waits for them, and re-layouts  2.19 us (3%)
    pallas_call x1, Pallas kernels, gradients(): pl.pallas_call(functools.partial(gradients_kernel, shape), in_specs=[pl.B...  67.7 us
    dot_general x1, matrix products, body(): jnp.einsum('rc,dc->rd', grad_kv, weight, preferred_element_type=jnp.float32)  7.38 us
    unnamed x6, local copies, waits for them, and re-layouts  2.19 us

commit v1 on v0

--- a/solution.py
+++ b/solution.py
@@ -303,11 +303,11 @@
     return pl.pallas_call(
         functools.partial(gradients_kernel, shape),
         in_specs=[pl.BlockSpec(memory_space=pltpu.SMEM)] + [pl.BlockSpec(memory_space=pltpu.HBM)] * 4,
-        out_specs=[vmem, vmem, pl.BlockSpec(memory_space=pl.ANY)],
+        out_specs=[pl.BlockSpec(memory_space=pltpu.VMEM)]*3,
         out_shape=[
-            jax.ShapeDtypeStruct((rows, width), jnp.bfloat16),
-            jax.ShapeDtypeStruct((rows, columns), jnp.bfloat16),
-            jax.ShapeDtypeStruct((w_rows * shards * count, columns), jnp.bfloat16),
+            pltpu.VMEM((rows, width), jnp.bfloat16),
+            pltpu.VMEM((rows, columns), jnp.bfloat16),
+            pltpu.VMEM((w_rows * shards * count, columns), jnp.bfloat16),
         ],
         scratch_shapes=[
             pltpu.VMEM((rows, width), jnp.bfloat16),
@@ -335,9 +335,47 @@
             dma,
         ],
         compiler_params=pltpu.CompilerParams(
-            vmem_limit_bytes=67043328, collective_id=0, has_side_effects=True
+            vmem_limit_bytes=53*1024*1024, collective_id=0, has_side_effects=True
         ),
     )(lengths, query, grad, kv0, w_own)
+
+
+def finish_kernel(q_ref, kv_ref, w_ref, q_out, kv_out, in_out, buf, sems):
+    chunks = sems.shape[0] - 2
+    step = buf.shape[1] // chunks
+    qc = pltpu.make_async_copy(q_ref, q_out, sems.at[chunks])
+    kc = pltpu.make_async_copy(kv_ref, kv_out, sems.at[chunks + 1])
+    qc.start()
+    kc.start()
+    def cp(n):
+        cols = pl.ds(n * step, step)
+        return pltpu.make_async_copy(buf.at[:, cols], in_out.at[:, cols], sems.at[n])
+    for n in range(chunks):
+        buf[:, n * step:(n + 1) * step] = dot(kv_ref[...], w_ref[n * step:(n + 1) * step, :], ((1,), (1,))).astype(jnp.bfloat16)
+        cp(n).start()
+    for n in range(chunks):
+        cp(n).wait()
+    qc.wait()
+    kc.wait()
+
+
+def finish(grad_query, grad_kv, weight):
+    rows, width = grad_query.shape
+    feats = weight.shape[0]
+    anyspec = pl.BlockSpec(memory_space=pl.ANY)
+    vm = pl.BlockSpec(memory_space=pltpu.VMEM)
+    return pl.pallas_call(
+        finish_kernel,
+        in_specs=[vm, vm, vm],
+        out_specs=[anyspec] * 3,
+        out_shape=[
+            jax.ShapeDtypeStruct((rows, width), jnp.bfloat16),
+            jax.ShapeDtypeStruct(grad_kv.shape, jnp.bfloat16),
+            jax.ShapeDtypeStruct((rows, feats), jnp.bfloat16),
+        ],
+        scratch_shapes=[pltpu.VMEM((rows, feats), jnp.bfloat16), pltpu.SemaphoreType.DMA((10,))],
+        compiler_params=pltpu.CompilerParams(vmem_limit_bytes=20*1024*1024),
+    )(grad_query, grad_kv, weight)
 
 
 def body(query, key_value_rows, grad_out, doc_lengths, key_value_weight):
@@ -345,8 +383,8 @@
     grad_query, grad_kv, weight = gradients(
         shape, doc_lengths, query[0], grad_out[0], key_value_rows[0], key_value_weight
     )
-    grad_input = jnp.einsum("rc,dc->rd", grad_kv, weight, preferred_element_type=jnp.float32)
-    return (grad_query[None], grad_kv[None], grad_input.astype(jnp.bfloat16)[None])
+    grad_query, grad_kv, grad_input = finish(grad_query, grad_kv, weight)
+    return (grad_query[None], grad_kv[None], grad_input[None])
 
 
 def solution(mesh):

time: 78.1 us -> 69.3 us (0.89)
  matrix products: 7.38 us -> 0 us
  local copies, waits for them, and re-layouts: 2.19 us -> 0 us
  Pallas kernels: 67.7 us -> 68.5 us
    dot_general x1 -> x0, matrix products: 7.38 us -> none  [body(): jnp.einsum('rc,dc->rd', grad_kv, weight, preferred_element_type=jnp.float32)]
    pallas_call x0 -> x1, Pallas kernels: none -> 3.17 us  [finish(): pl.pallas_call(finish_kernel, in_specs=[vm, vm, vm], out_specs=[anyspec]...]
    pallas_call x1, Pallas kernels: 67.7 us -> 65.4 us  [gradients(): pl.pallas_call(functools.partial(gradients_kernel, shape), in_specs=[pl.B...]
    unnamed x6 -> x0, local copies, waits for them, and re-layouts: 2.19 us -> none
where the time goes in v1:
time: 69.3 us; the launch traced here: 69.2 us
  Pallas kernels  68.5 us (99%)
    pallas_call x1, Pallas kernels, gradients(): pl.pallas_call(functools.partial(gradients_kernel, shape), in_specs=[pl.B...  65.4 us
    pallas_call x1, Pallas kernels, finish(): pl.pallas_call(finish_kernel, in_specs=[vm, vm, vm], out_specs=[anyspec]...  3.17 us

profile of v1, /device:TPU:25, one launch (start us, length us, event | category | flops | bytes accessed | tf_op | source)
XLA Modules:
  0.0 69.2 jit_solution(14859686746098457906)
XLA Ops:
  0.6 65.4 %shard_map.76 = (bf16[256,4096]{1,0:T(8,128)(2,1)S(1)}, bf16[256,1024]{1,0:T(8,128)(2,1)S(1)}, bf16[4096,1024]{1,0:T(8,128)(2,1)S(1)}) custom-call(s32[1,8]{1,0:T(1,128)} %lengths.1, bf16[256,4096]{1,0:T(8,128)(2,1)} %bitcast.6, bf16[256,4096]{1,0:T(8,128)(2,1)} %bitcast.7, bf16[256,1024]{1,0:T(8,128)(2,1)} %bitcast.8, bf16[128,1024]{1,0:T(8,128)(2,1)} %w_own.1), custom_call_target="tpu_custom_call" | custom-call | tf_op jit(solution)/shard_map/pallas_call | solution.py:303
  66.0 3.2 %shard_map.77 = (bf16[256,4096]{1,0:T(8,128)(2,1)}, bf16[256,1024]{1,0:T(8,128)(2,1)}, bf16[256,4096]{1,0:T(8,128)(2,1)}) custom-call(bf16[256,4096]{1,0:T(8,128)(2,1)S(1)} %get-tuple-element.9.q_ref, bf16[256,1024]{1,0:T(8,128)(2,1)S(1)} %get-tuple-element.10.kv_ref, bf16[4096,1024]{1,0:T(8,128)(2,1)S(1)} %get-tuple-element.11.w_ref), custom_call_target="tpu_custom_call" | custom-call | tf_op jit(solution)/shard_map/pallas_call | solution.py:367

commit v2 on v1

--- a/solution.py
+++ b/solution.py
@@ -12,6 +12,7 @@
 HEAD_SIZE = 128
 DOC_SHARDS = 2
 GROUP = QUERY_HEAD_COUNT // KEY_VALUE_HEADS
+STEP = 2
 LOG2E = 1.4426950408889634
 
 
@@ -340,6 +341,519 @@
     )(lengths, query, grad, kv0, w_own)
 
 
+def plan_of(shards):
+    return {
+        "start": (("kv", 0), ("kv", 1), ("kv", 2), ("own", 0), ("kv", 3),),
+        "early": (("line", 1), ("line", 2),),
+        (0, 2): (("line", 3), ("y", 0),),
+        (1, 0): (("x", 0),),
+        (1, 1): (("y", 1),),
+        (1, 2): (("x", 1),),
+        (2, 0): (("y", 2),),
+        (2, 1): (("by", 1), ("py", 1), ("by", 2), ("py", 2),),
+        (2, 3): (("y", 3), ("bx", 1), ("px", 1), ("x", 3), ("x", 2), ("bx", 2), ("px", 2), ("d", 0),),
+        "after": (("d", 3), ("by", 3), ("py", 3), ("bd", 1), ("bd", 2), ("d", 2), ("pd", 2), ("bx", 3), ("px", 3), ("bd", 3), ("pd", 3), ("d", 1), ("pd", 1),),
+    }
+
+
+def plane_kernel(
+    shape, plan, lengths, query_hbm, grad_hbm, kv_hbm, w_own, grad_query, grad_kv, w_all,
+    query, grad, kv0, in_sem, kv_sem,
+    window, near, far, landed_near, landed_far, own, rest, bias, dk, dv,
+    kv_send, kv_recv, g_send, g_recv, line_send, line_recv, side_send, side_recv,
+    diag_send, diag_recv, tail_send, tail_recv, pair_send, pair_recv, local_sem,
+):
+    shards, count = shape
+    chips = count // 2
+    rows = query.shape[0]
+    half = rows // 2
+    group_width = GROUP * HEAD_SIZE
+    w_rows = w_own.shape[0]
+    part_one = w_rows * 32 // 128
+    part_two = w_rows * 80 // 128
+    keys = (DOC_SHARDS + 1) * rows
+    scale = HEAD_SIZE ** (-0.5)
+    z = lax.axis_index("fsdp")
+    me = lax.axis_index("ctx")
+    core = lax.rem(me, 2)
+    chip = me // 2
+    x = lax.rem(chip, 2)
+    y = chip // 2
+    even = x == y
+    x_peer = me + 2 - 4 * x
+    y_peer = me + 4 - 8 * y
+    d_peer = x_peer + 4 - 8 * y
+    sides = (x_peer, y_peer, d_peer)
+    partner = me + 1 - 2 * core
+    has_prev = chip >= 1
+    has_next = chip < chips - 1
+    up = lax.rem(z + 1, shards)
+    down = lax.rem(z - 1 + shards, shards)
+
+    def query_in(g):
+        cols = pl.ds(pl.multiple_of(g * group_width, HEAD_SIZE), group_width)
+        return pltpu.make_async_copy(query_hbm.at[:, cols], query.at[:, cols], in_sem.at[0, g])
+
+    def grad_in(g):
+        cols = pl.ds(pl.multiple_of(g * group_width, HEAD_SIZE), group_width)
+        return pltpu.make_async_copy(grad_hbm.at[:, cols], grad.at[:, cols], in_sem.at[1, g])
+
+    kv_in = pltpu.make_async_copy(kv_hbm, kv0, kv_sem)
+    kv_in.start()
+    for g in range(KEY_VALUE_HEADS):
+        query_in(g).start()
+        grad_in(g).start()
+
+    barrier = pltpu.get_barrier_semaphore()
+    peers = [(z, partner), (z, x_peer), (z, y_peer), (z, d_peer), (up, me), (down, me)]
+    for peer in peers:
+        pl.semaphore_signal(barrier, inc=1, device_id=peer, device_id_type=pl.DeviceIdType.MESH)
+    pl.semaphore_wait(barrier, len(peers))
+
+    def remote(src, dst, send, recv, device):
+        return pltpu.make_async_remote_copy(
+            src_ref=src, dst_ref=dst, send_sem=send, recv_sem=recv,
+            device_id=device, device_id_type=pl.DeviceIdType.MESH,
+        )
+
+    def kv_cols(g, part):
+        return pl.ds(pl.multiple_of((part * KEY_VALUE_HEADS + g) * HEAD_SIZE, HEAD_SIZE), HEAD_SIZE)
+
+    def kv_far(g, part):
+        cols = kv_cols(g, part)
+        return remote(
+            kv_hbm.at[:, cols], window.at[1, :, cols], kv_send.at[1, g, part], kv_recv.at[1, g, part],
+            (z, lax.rem(me + 2, count)),
+        )
+
+    def kv_near(g, part):
+        cols = kv_cols(g, part)
+        return remote(
+            kv_hbm.at[:, cols], window.at[0, :, cols], kv_send.at[0, g, part], kv_recv.at[0, g, part],
+            (z, partner),
+        )
+
+    def kv_relay(g, part):
+        cols = kv_cols(g, part)
+        return remote(
+            window.at[1, :, cols], window.at[0, :, cols], kv_send.at[0, g, part], kv_recv.at[0, g, part],
+            (z, partner),
+        )
+
+    def near_copy(g):
+        return remote(near.at[g], landed_near.at[g], g_send.at[0, g], g_recv.at[0, g], (z, partner))
+
+    def far_copy(g):
+        return remote(
+            far.at[g], landed_far.at[g], g_send.at[1, g], g_recv.at[1, g],
+            (z, lax.rem(me - 2 + count, count)),
+        )
+
+    def block(zz, c, first=0, last=None):
+        size = (w_rows if last is None else last) - first
+        return w_all.at[pl.ds(pl.multiple_of((zz * count + c) * w_rows + first, 8), size)]
+
+    def line(zz, way, mine=False):
+        device = (up if way == 0 else down, me)
+        return remote(
+            w_own if mine else block(zz, me), block(zz, me), line_send.at[way, zz], line_recv.at[zz], device
+        )
+
+    def side(k, zz, mine=False):
+        last = w_rows if mine else part_two
+        src = w_own if mine else block(zz, me, 0, last)
+        return remote(
+            src, block(zz, me, 0, last), side_send.at[k, zz], side_recv.at[k, zz], (z, sides[k])
+        )
+
+    def side_wait(k, zz, whole):
+        last = w_rows if whole else part_two
+        ref = block(zz, sides[k], 0, last)
+        remote(ref, ref, side_send.at[k, zz], side_recv.at[k, zz], (z, sides[k])).wait_recv()
+
+    def diag_two(zz, whole):
+        ref = block(zz, x_peer, part_one, w_rows if whole else part_two)
+        return remote(ref, ref, diag_send.at[1, zz], diag_recv.at[1, zz], (z, y_peer))
+
+    def diag_one(zz, over_x):
+        ref = block(zz, y_peer if over_x else x_peer, 0, part_one)
+        device = (z, x_peer if over_x else y_peer)
+        return remote(ref, ref, diag_send.at[0, zz], diag_recv.at[0, zz], device)
+
+    def diag_wait(zz, whole):
+        ref = block(zz, d_peer, 0, part_one)
+        remote(ref, ref, diag_send.at[0, zz], diag_recv.at[0, zz], (z, y_peer)).wait_recv()
+        ref = block(zz, d_peer, part_one, w_rows if whole else part_two)
+        remote(ref, ref, diag_send.at[1, zz], diag_recv.at[1, zz], (z, y_peer)).wait_recv()
+
+    def tail(k, zz, way):
+        ref = block(zz, sides[k], part_two, w_rows)
+        device = (up if way == 0 else down, me)
+        return remote(ref, ref, tail_send.at[way, k, zz], tail_recv.at[k, zz], device)
+
+    def pair(k, zz, mine=False):
+        ref = block(zz, me if k == 3 else sides[k])
+        return remote(
+            w_own if mine else ref, ref, pair_send.at[k, zz], pair_recv.at[k, zz], (z, partner)
+        )
+
+    shorter = jnp.minimum(z, shards - 1 - z)
+    longer = jnp.where(z < shards - 1 - z, 1, -1)
+
+    def source(i):
+        near_side = i <= 2 * shorter
+        sign = jnp.where(near_side, 1 if i % 2 == 1 else -1, longer)
+        distance = jnp.where(near_side, (i + 1) // 2, i - shorter)
+        return z + sign * distance, sign
+
+    def start(copy):
+        copy.start()
+
+    def finish(copy):
+        copy.wait_send()
+
+    def onward(make, sign, act):
+        @pl.when((sign < 0) & (z < shards - 1))
+        def _():
+            act(make(0))
+
+        @pl.when((sign > 0) & (z > 0))
+        def _():
+            act(make(1))
+
+    def both_ways(make, act):
+        @pl.when(z < shards - 1)
+        def _():
+            act(make(0))
+
+        @pl.when(z > 0)
+        def _():
+            act(make(1))
+
+    def own_line(act):
+        both_ways(lambda way: line(z, way, True), act)
+
+    def relay_x(zz, whole, act):
+        act(diag_two(zz, whole))
+
+        @pl.when(jnp.logical_not(even))
+        def _():
+            act(diag_one(zz, False))
+
+    def relay_y(zz, act):
+        @pl.when(even)
+        def _():
+            act(diag_one(zz, True))
+
+    def event(kind, i, wait, act):
+        if kind == "kv":
+            @pl.when(has_next)
+            def _():
+                for part in range(2):
+                    act(kv_far(i, part))
+            return
+        if kind == "own":
+            own_line(act)
+            act(side(1, z, True))
+            act(side(0, z, True))
+            return
+        zz, sign = (z, 0) if i == 0 else source(i)
+        if kind == "line":
+            if wait:
+                remote(block(zz, me), block(zz, me), line_send.at[0, zz], line_recv.at[zz], (up, me)).wait_recv()
+            onward(lambda way: line(zz, way), sign, act)
+            act(side(1, zz))
+            act(side(0, zz))
+            act(pair(3, zz))
+        elif kind == "x":
+            if wait:
+                side_wait(0, zz, i == 0)
+            relay_x(zz, i == 0, act)
+            if i == 0:
+                both_ways(lambda way: tail(0, zz, way), act)
+                act(pair(0, zz))
+        elif kind == "y":
+            if wait:
+                side_wait(1, zz, i == 0)
+            relay_y(zz, act)
+            if i == 0:
+                both_ways(lambda way: tail(1, zz, way), act)
+                act(pair(1, zz))
+        elif kind == "d":
+            if wait:
+                diag_wait(zz, i == 0)
+            if i == 0:
+                both_ways(lambda way: tail(2, zz, way), act)
+                act(pair(2, zz))
+        elif kind in ("bx", "by", "bd"):
+            k = ("bx", "by", "bd").index(kind)
+            if wait:
+                ref = block(zz, sides[k], part_two, w_rows)
+                remote(ref, ref, tail_send.at[0, k, zz], tail_recv.at[k, zz], (up, me)).wait_recv()
+            onward(lambda way: tail(k, zz, way), sign, act)
+        elif kind in ("px", "py", "pd"):
+            act(pair(("px", "py", "pd").index(kind), zz))
+
+    def serve(events):
+        for kind, i in events:
+            event(kind, i, True, start)
+
+    def kv_forward(g):
+        @pl.when(has_prev)
+        def _():
+            for part in range(2):
+                kv_far(g, part).wait_recv()
+
+        @pl.when(has_prev & (core == 1))
+        def _():
+            for part in range(2):
+                kv_relay(g, part).start()
+
+    serve(plan["start"])
+    for g in range(KEY_VALUE_HEADS):
+        @pl.when(core == 0)
+        def _():
+            for part in range(2):
+                kv_near(g, part).start()
+    pair(3, z, True).start()
+    local = pltpu.make_async_copy(w_own, block(z, me), local_sem)
+    local.start()
+
+    @pl.when(me < 1)
+    def _():
+        window[0] = jnp.zeros(window.shape[1:], window.dtype)
+
+    @pl.when(me < 2)
+    def _():
+        window[1] = jnp.zeros(window.shape[1:], window.dtype)
+
+    first = me * rows
+    pos = first + lax.broadcasted_iota(jnp.int32, (1, rows), 1)
+    begin = jnp.zeros((1, rows), jnp.int32)
+    end = jnp.int32(0)
+    for d in range(lengths.shape[1]):
+        end = end + lengths[0, d]
+        begin = jnp.where(pos >= end, end, begin)
+    key_pos = first - DOC_SHARDS * rows + lax.broadcasted_iota(jnp.int32, (keys, rows), 0)
+    live = (key_pos >= begin) & (key_pos <= pos)
+    bias[...] = jnp.where(live, 0.0, -1e30)
+
+    def send_far(g):
+        @pl.when(has_prev & (core == 1))
+        def _():
+            near_copy(g).wait_recv()
+            for part in range(2):
+                far[g, part] = (rest[part] + landed_near[g, part].astype(jnp.float32)).astype(jnp.bfloat16)
+
+        @pl.when(has_prev & (core == 0))
+        def _():
+            for part in range(2):
+                far[g, part] = rest[part].astype(jnp.bfloat16)
+
+        @pl.when(has_prev)
+        def _():
+            far_copy(g).start()
+
+    def blocks(a):
+        return a[:half, :half], a[half:keys - half], a[keys - half:, half:]
+
+    def joined(top, middle, bottom):
+        empty = jnp.zeros((half, half), top.dtype)
+        return jnp.concatenate(
+            [jnp.concatenate([top, empty], axis=1), middle, jnp.concatenate([empty, bottom], axis=1)], axis=0
+        )
+
+    def column_sum(top, middle, bottom):
+        total = jnp.sum(middle, axis=0, keepdims=True)
+        return total + jnp.concatenate(
+            [jnp.sum(top, axis=0, keepdims=True), jnp.sum(bottom, axis=0, keepdims=True)], axis=1
+        )
+
+    def split(row):
+        return row[:, :half], row, row[:, half:]
+
+    def heads(g, which, key, value):
+        all_p, all_ds, all_q, all_go = [], [], [], []
+        for h in which:
+            cols = pl.ds(pl.multiple_of((g * GROUP + h) * HEAD_SIZE, HEAD_SIZE), HEAD_SIZE)
+            q = query[:, cols]
+            go = grad[:, cols]
+            s = dot(key, q, ((1,), (1,)))
+            dp = blocks(dot(value, go, ((1,), (1,))))
+            b = (bias[:half, :half], bias[half:keys - half, :], bias[keys - half:, half:])
+            e = [jnp.exp2(si * (scale * LOG2E) + bi) for si, bi in zip(blocks(s), b)]
+            inv = 1.0 / column_sum(*e)
+            delta = column_sum(*[ei * di for ei, di in zip(e, dp)]) * inv
+            p = [ei * ii for ei, ii in zip(e, split(inv))]
+            ds = [(pi * (di - li)).astype(jnp.bfloat16) for pi, di, li in zip(p, dp, split(delta))]
+            all_p.append(joined(*[pi.astype(jnp.bfloat16) for pi in p]))
+            all_ds.append(joined(*ds))
+            all_q.append(q)
+            all_go.append(go)
+        p = jnp.concatenate(all_p, axis=1)
+        ds = jnp.concatenate(all_ds, axis=1)
+        return (
+            dot(p, jnp.concatenate(all_go, axis=0), ((1,), (0,))),
+            dot(ds, jnp.concatenate(all_q, axis=0), ((1,), (0,))),
+            dot(key, ds, ((0,), (0,))),
+        )
+
+    def group(g, carry):
+        @pl.when(me >= 1)
+        def _():
+            for part in range(2):
+                kv_near(g, part).wait_recv()
+        query_in(g).wait()
+        grad_in(g).wait()
+
+        kc = pl.ds(pl.multiple_of(g * HEAD_SIZE, HEAD_SIZE), HEAD_SIZE)
+        vc = pl.ds(pl.multiple_of((g + KEY_VALUE_HEADS) * HEAD_SIZE, HEAD_SIZE), HEAD_SIZE)
+        for n in range(0, GROUP, STEP):
+            key = jnp.concatenate([window[1, :, kc], window[0, :, kc], kv0[:, kc]], axis=0)
+            value = jnp.concatenate([window[1, :, vc], window[0, :, vc], kv0[:, vc]], axis=0)
+            dv_part, dk_part, dq = heads(g, range(n, n + STEP), key, value)
+            if n == 0:
+                dv[...] = dv_part
+                dk[...] = dk_part
+            else:
+                dv[...] += dv_part
+                dk[...] += dk_part
+            for j in range(STEP):
+                cols = pl.ds(pl.multiple_of((g * GROUP + n + j) * HEAD_SIZE, HEAD_SIZE), HEAD_SIZE)
+                grad_query[:, cols] = (dq[:, j * rows:(j + 1) * rows] * scale).T.astype(jnp.bfloat16)
+            if n == 0:
+                @pl.when(g >= 1)
+                def _():
+                    send_far(g - 1)
+            if n == GROUP - STEP:
+                @pl.when(g < KEY_VALUE_HEADS - 1)
+                def _():
+                    kv_forward(g + 1)
+            for k in range(KEY_VALUE_HEADS):
+                events = plan.get((k, n // STEP), ())
+                if events:
+                    @pl.when(g == k)
+                    def _():
+                        serve(events)
+        near[g, 0] = (dk[rows:2 * rows, :] * scale).astype(jnp.bfloat16)
+        near[g, 1] = dv[rows:2 * rows, :].astype(jnp.bfloat16)
+
+        @pl.when(me >= 1)
+        def _():
+            near_copy(g).start()
+        rest[0] = dk[:rows, :] * scale
+        rest[1] = dv[:rows, :]
+        own[g, 0] = dk[2 * rows:, :] * scale
+        own[g, 1] = dv[2 * rows:, :]
+        return carry
+
+    serve(plan["early"])
+    kv_forward(0)
+    kv_in.wait()
+    lax.fori_loop(0, KEY_VALUE_HEADS, group, 0)
+    send_far(KEY_VALUE_HEADS - 1)
+    serve(plan["after"])
+
+    for g in range(KEY_VALUE_HEADS):
+        @pl.when(core == 0)
+        def _():
+            near_copy(g).wait_recv()
+            for part in range(2):
+                own[g, part] += landed_near[g, part].astype(jnp.float32)
+
+        @pl.when(has_next)
+        def _():
+            far_copy(g).wait_recv()
+            for part in range(2):
+                own[g, part] += landed_far[g, part].astype(jnp.float32)
+        for part in range(2):
+            at = (part * KEY_VALUE_HEADS + g) * HEAD_SIZE
+            grad_kv[:, at:at + HEAD_SIZE] = own[g, part].astype(jnp.bfloat16)
+
+    for k in range(4):
+        for zz in range(shards):
+            ref = block(zz, partner if k == 3 else sides[k] + 1 - 2 * core)
+            remote(ref, ref, pair_send.at[k, zz], pair_recv.at[k, zz], (z, partner)).wait_recv()
+
+    pair(3, z, True).wait_send()
+    for events in plan.values():
+        for kind, i in events:
+            event(kind, i, False, finish)
+    local.wait()
+    for g in range(KEY_VALUE_HEADS):
+        for part in range(2):
+            @pl.when(core == 0)
+            def _():
+                kv_near(g, part).wait_send()
+
+            @pl.when(has_prev & (core == 1))
+            def _():
+                kv_relay(g, part).wait_send()
+
+        @pl.when(me >= 1)
+        def _():
+            near_copy(g).wait_send()
+
+        @pl.when(has_prev)
+        def _():
+            far_copy(g).wait_send()
+
+
+def plane_gradients(shape, lengths, query, grad, kv0, w_own):
+    rows, width = query.shape
+    keys = (DOC_SHARDS + 1) * rows
+    w_rows, columns = w_own.shape
+    shards, count = shape
+    dma = pltpu.SemaphoreType.DMA
+    terms = (KEY_VALUE_HEADS, 2, rows, HEAD_SIZE)
+    operands = [pltpu.with_memory_space_constraint(a, pltpu.HBM) for a in (query, grad, kv0, w_own)]
+    return pl.pallas_call(
+        functools.partial(plane_kernel, shape, plan_of(shards)),
+        in_specs=[pl.BlockSpec(memory_space=pltpu.SMEM)] + [pl.BlockSpec(memory_space=pltpu.HBM)] * 4,
+        out_specs=[pl.BlockSpec(memory_space=pltpu.VMEM)] * 3,
+        out_shape=[
+            pltpu.VMEM((rows, width), jnp.bfloat16),
+            pltpu.VMEM((rows, columns), jnp.bfloat16),
+            pltpu.VMEM((w_rows * shards * count, columns), jnp.bfloat16),
+        ],
+        scratch_shapes=[
+            pltpu.VMEM((rows, width), jnp.bfloat16),
+            pltpu.VMEM((rows, width), jnp.bfloat16),
+            pltpu.VMEM((rows, columns), jnp.bfloat16),
+            dma((2, KEY_VALUE_HEADS)),
+            dma,
+            pltpu.VMEM((DOC_SHARDS, rows, columns), jnp.bfloat16),
+            pltpu.VMEM(terms, jnp.bfloat16),
+            pltpu.VMEM(terms, jnp.bfloat16),
+            pltpu.VMEM(terms, jnp.bfloat16),
+            pltpu.VMEM(terms, jnp.bfloat16),
+            pltpu.VMEM(terms, jnp.float32),
+            pltpu.VMEM(terms[1:], jnp.float32),
+            pltpu.VMEM((keys, rows), jnp.float32),
+            pltpu.VMEM((keys, HEAD_SIZE), jnp.float32),
+            pltpu.VMEM((keys, HEAD_SIZE), jnp.float32),
+            dma((DOC_SHARDS, KEY_VALUE_HEADS, 2)),
+            dma((DOC_SHARDS, KEY_VALUE_HEADS, 2)),
+            dma((2, KEY_VALUE_HEADS)),
+            dma((2, KEY_VALUE_HEADS)),
+            dma((2, shards)),
+            dma((shards,)),
+            dma((2, shards)),
+            dma((2, shards)),
+            dma((2, shards)),
+            dma((2, shards)),
+            dma((2, 3, shards)),
+            dma((3, shards)),
+            dma((4, shards)),
+            dma((4, shards)),
+            dma,
+        ],
+        compiler_params=pltpu.CompilerParams(
+            vmem_limit_bytes=50 * 1024 * 1024, collective_id=1, has_side_effects=True
+        ),
+    )(lengths, *operands)
+
+
 def finish_kernel(q_ref, kv_ref, w_ref, q_out, kv_out, in_out, buf, sems):
     chunks = sems.shape[0] - 2
     step = buf.shape[1] // chunks
@@ -380,7 +894,8 @@
 
 def body(query, key_value_rows, grad_out, doc_lengths, key_value_weight):
     shape = (lax.axis_size("fsdp"), lax.axis_size("ctx"))
-    grad_query, grad_kv, weight = gradients(
+    run = plane_gradients if shape[0] == 4 and shape[1] == 8 else gradients
+    grad_query, grad_kv, weight = run(
         shape, doc_lengths, query[0], grad_out[0], key_value_rows[0], key_value_weight
     )
     grad_query, grad_kv, grad_input = finish(grad_query, grad_kv, weight)

time: 69.3 us -> 60.9 us (0.88)
  the two profiles are of different devices: /device:TPU:25 before, /device:TPU:5 now
where the time goes in v2:
time: 60.9 us; the launch traced here: 59.8 us
  Pallas kernels  59.1 us (97%)
  between operations  0.64 us (1%)
    pallas_call x1, Pallas kernels, plane_gradients(): pl.pallas_call(functools.partial(plane_kernel, shape, plan_of(shards)), i...  56 us
    pallas_call x1, Pallas kernels, finish(): pl.pallas_call(finish_kernel, in_specs=[vm, vm, vm], out_specs=[anyspec]...  3.17 us

profile of v2, /device:TPU:5, one launch (start us, length us, event | category | flops | bytes accessed | tf_op | source)
XLA Modules:
  0.0 59.8 jit_solution(2289635500945228806)
XLA Ops:
  0.6 56.0 %shard_map.76 = (bf16[256,4096]{1,0:T(8,128)(2,1)S(1)}, bf16[256,1024]{1,0:T(8,128)(2,1)S(1)}, bf16[4096,1024]{1,0:T(8,128)(2,1)S(1)}) custom-call(s32[1,8]{1,0:T(1,128)} %lengths.1, bf16[256,4096]{1,0:T(8,128)(2,1)} %bitcast.6, bf16[256,4096]{1,0:T(8,128)(2,1)} %bitcast.7, bf16[256,1024]{1,0:T(8,128)(2,1)} %bitcast.8, bf16[128,1024]{1,0:T(8,128)(2,1)} %w_own.1), custom_call_target="tpu_custom_call" | custom-call | tf_op jit(solution)/shard_map/pallas_call | solution.py:810
  56.6 3.2 %shard_map.77 = (bf16[256,4096]{1,0:T(8,128)(2,1)}, bf16[256,1024]{1,0:T(8,128)(2,1)}, bf16[256,4096]{1,0:T(8,128)(2,1)}) custom-call(bf16[256,4096]{1,0:T(8,128)(2,1)S(1)} %get-tuple-element.9.q_ref, bf16[256,1024]{1,0:T(8,128)(2,1)S(1)} %get-tuple-element.10.kv_ref, bf16[4096,1024]{1,0:T(8,128)(2,1)S(1)} %get-tuple-element.11.w_ref), custom_call_target="tpu_custom_call" | custom-call | tf_op jit(solution)/shard_map/pallas_call | solution.py:881

commit v3 on v2

--- a/solution.py
+++ b/solution.py
@@ -343,16 +343,62 @@
 
 def plan_of(shards):
     return {
-        "start": (("kv", 0), ("kv", 1), ("kv", 2), ("own", 0), ("kv", 3),),
-        "early": (("line", 1), ("line", 2),),
-        (0, 2): (("line", 3), ("y", 0),),
-        (1, 0): (("x", 0),),
-        (1, 1): (("y", 1),),
-        (1, 2): (("x", 1),),
-        (2, 0): (("y", 2),),
-        (2, 1): (("by", 1), ("py", 1), ("by", 2), ("py", 2),),
-        (2, 3): (("y", 3), ("bx", 1), ("px", 1), ("x", 3), ("x", 2), ("bx", 2), ("px", 2), ("d", 0),),
-        "after": (("d", 3), ("by", 3), ("py", 3), ("bd", 1), ("bd", 2), ("d", 2), ("pd", 2), ("bx", 3), ("px", 3), ("bd", 3), ("pd", 3), ("d", 1), ("pd", 1),),
+        "start": (
+            (("kv", 0), ("kv", 1), ("own", 0), ("kv", 2), ("kv", 3),),
+            (("kv", 0), ("own", 0), ("kv", 1), ("kv", 2),),
+        ),
+        "early": (
+            (("y", 0), ("line", 1), ("line", 2),),
+            (("line", 1),),
+        ),
+        (0, 2): (
+            (),
+            (("y", 0), ("x", 0), ("kv", 3),),
+        ),
+        (0, 3): (
+            (("x", 0),),
+            (),
+        ),
+        (1, 1): (
+            (("line", 3),),
+            (),
+        ),
+        (1, 2): (
+            (("bx", 2), ("by", 2),),
+            (("line", 2),),
+        ),
+        (2, 0): (
+            (("by", 1), ("x", 1),),
+            (),
+        ),
+        (2, 1): (
+            (("d", 0),),
+            (("by", 1), ("x", 1), ("d", 0),),
+        ),
+        (2, 2): (
+            (("y", 1), ("py", 1),),
+            (("line", 3),),
+        ),
+        (2, 3): (
+            (("bx", 1), ("px", 1),),
+            (),
+        ),
+        (3, 0): (
+            (("bd", 2), ("x", 2), ("px", 2), ("y", 2), ("py", 2), ("by", 3),),
+            (),
+        ),
+        (3, 1): (
+            (),
+            (("x", 2), ("y", 1), ("py", 1),),
+        ),
+        (3, 2): (
+            (("x", 3), ("y", 3), ("py", 3), ("bd", 1),),
+            (),
+        ),
+        "after": (
+            (("bx", 3), ("px", 3), ("bd", 3), ("d", 3), ("pd", 3), ("d", 1), ("pd", 1), ("d", 2), ("pd", 2),),
+            (("by", 2), ("x", 3), ("y", 2), ("py", 2), ("y", 3), ("by", 3), ("py", 3), ("bx", 1), ("px", 1), ("d", 3), ("bx", 2), ("px", 2), ("bd", 1), ("bx", 3), ("px", 3), ("bd", 3), ("pd", 3), ("bd", 2), ("d", 2), ("pd", 2), ("d", 1), ("pd", 1),),
+        ),
     }
 
 
@@ -369,7 +415,7 @@
     half = rows // 2
     group_width = GROUP * HEAD_SIZE
     w_rows = w_own.shape[0]
-    part_one = w_rows * 32 // 128
+    part_one = w_rows * 56 // 128
     part_two = w_rows * 80 // 128
     keys = (DOC_SHARDS + 1) * rows
     scale = HEAD_SIZE ** (-0.5)
@@ -594,9 +640,15 @@
         elif kind in ("px", "py", "pd"):
             act(pair(("px", "py", "pd").index(kind), zz))
 
-    def serve(events):
-        for kind, i in events:
-            event(kind, i, True, start)
+    at_end = (z == 0) | (z == shards - 1)
+
+    def serve(key, now=True):
+        for place, events in zip((jnp.logical_not(at_end), at_end), plan.get(key, ((), ()))):
+            if events:
+                @pl.when(place & now)
+                def _():
+                    for kind, i in events:
+                        event(kind, i, True, start)
 
     def kv_forward(g):
         @pl.when(has_prev)
@@ -609,7 +661,7 @@
             for part in range(2):
                 kv_relay(g, part).start()
 
-    serve(plan["start"])
+    serve("start")
     for g in range(KEY_VALUE_HEADS):
         @pl.when(core == 0)
         def _():
@@ -730,11 +782,7 @@
                 def _():
                     kv_forward(g + 1)
             for k in range(KEY_VALUE_HEADS):
-                events = plan.get((k, n // STEP), ())
-                if events:
-                    @pl.when(g == k)
-                    def _():
-                        serve(events)
+                serve((k, n // STEP), g == k)
         near[g, 0] = (dk[rows:2 * rows, :] * scale).astype(jnp.bfloat16)
         near[g, 1] = dv[rows:2 * rows, :].astype(jnp.bfloat16)
 
@@ -747,12 +795,12 @@
         own[g, 1] = dv[2 * rows:, :]
         return carry
 
-    serve(plan["early"])
+    serve("early")
     kv_forward(0)
     kv_in.wait()
     lax.fori_loop(0, KEY_VALUE_HEADS, group, 0)
     send_far(KEY_VALUE_HEADS - 1)
-    serve(plan["after"])
+    serve("after")
 
     for g in range(KEY_VALUE_HEADS):
         @pl.when(core == 0)
@@ -776,7 +824,7 @@
             remote(ref, ref, pair_send.at[k, zz], pair_recv.at[k, zz], (z, partner)).wait_recv()
 
     pair(3, z, True).wait_send()
-    for events in plan.values():
+    for events, _ in plan.values():
         for kind, i in events:
             event(kind, i, False, finish)
     local.wait()

time: 60.9 us -> 58.4 us (0.959)
  Pallas kernels: 59.1 us -> 56.9 us
    pallas_call x1, Pallas kernels: 56 us -> 53.7 us  [plane_gradients(): pl.pallas_call(functools.partial(plane_kernel, shape, plan_of(shards)), i...]
where the time goes in v3:
time: 58.4 us; the launch traced here: 57.5 us
  Pallas kernels  56.9 us (97%)
  between operations  0.64 us (1%)
    pallas_call x1, Pallas kernels, plane_gradients(): pl.pallas_call(functools.partial(plane_kernel, shape, plan_of(shards)), i...  53.7 us
    pallas_call x1, Pallas kernels, finish(): pl.pallas_call(finish_kernel, in_specs=[vm, vm, vm], out_specs=[anyspec]...  3.16 us

profile of v3, /device:TPU:5, one launch (start us, length us, event | category | flops | bytes accessed | tf_op | source)
XLA Modules:
  0.0 57.5 jit_solution(9960209636338499590)
XLA Ops:
  0.6 53.7 %shard_map.76 = (bf16[256,4096]{1,0:T(8,128)(2,1)S(1)}, bf16[256,1024]{1,0:T(8,128)(2,1)S(1)}, bf16[4096,1024]{1,0:T(8,128)(2,1)S(1)}) custom-call(s32[1,8]{1,0:T(1,128)} %lengths.1, bf16[256,4096]{1,0:T(8,128)(2,1)} %bitcast.6, bf16[256,4096]{1,0:T(8,128)(2,1)} %bitcast.7, bf16[256,1024]{1,0:T(8,128)(2,1)} %bitcast.8, bf16[128,1024]{1,0:T(8,128)(2,1)} %w_own.1), custom_call_target="tpu_custom_call" | custom-call | tf_op jit(solution)/shard_map/pallas_call | solution.py:858
  54.3 3.2 %shard_map.77 = (bf16[256,4096]{1,0:T(8,128)(2,1)}, bf16[256,1024]{1,0:T(8,128)(2,1)}, bf16[256,4096]{1,0:T(8,128)(2,1)}) custom-call(bf16[256,4096]{1,0:T(8,128)(2,1)S(1)} %get-tuple-element.9.q_ref, bf16[256,1024]{1,0:T(8,128)(2,1)S(1)} %get-tuple-element.10.kv_ref, bf16[4096,1024]{1,0:T(8,128)(2,1)S(1)} %get-tuple-element.11.w_ref), custom_call_target="tpu_custom_call" | custom-call | tf_op jit(solution)/shard_map/pallas_call | solution.py:929

commit v4 on v3

--- a/solution.py
+++ b/solution.py
@@ -344,7 +344,7 @@
 def plan_of(shards):
     return {
         "start": (
-            (("kv", 0), ("kv", 1), ("own", 0), ("kv", 2), ("kv", 3),),
+            (("kv", 0), ("own", 0), ("kv", 1), ("kv", 2), ("kv", 3),),
             (("kv", 0), ("own", 0), ("kv", 1), ("kv", 2),),
         ),
         "early": (

time: 58.4 us -> 56.1 us (0.961); the launches traced: 57.5 us -> 55.9 us
  Pallas kernels: 56.9 us -> 55.3 us
    pallas_call x1, Pallas kernels: 53.7 us -> 52.1 us  [plane_gradients(): pl.pallas_call(functools.partial(plane_kernel, shape, plan_of(shards)), i...]
where the time goes in v4:
time: 56.1 us; the launch traced here: 55.9 us
  Pallas kernels  55.3 us (99%)
  between operations  0.64 us (1%)
    pallas_call x1, Pallas kernels, plane_gradients(): pl.pallas_call(functools.partial(plane_kernel, shape, plan_of(shards)), i...  52.1 us
    pallas_call x1, Pallas kernels, finish(): pl.pallas_call(finish_kernel, in_specs=[vm, vm, vm], out_specs=[anyspec]...  3.17 us

profile of v4, /device:TPU:5, one launch (start us, length us, event | category | flops | bytes accessed | tf_op | source)
XLA Modules:
  0.0 55.9 jit_solution(9525025779354581685)
XLA Ops:
  0.6 52.1 %shard_map.76 = (bf16[256,4096]{1,0:T(8,128)(2,1)S(1)}, bf16[256,1024]{1,0:T(8,128)(2,1)S(1)}, bf16[4096,1024]{1,0:T(8,128)(2,1)S(1)}) custom-call(s32[1,8]{1,0:T(1,128)} %lengths.1, bf16[256,4096]{1,0:T(8,128)(2,1)} %bitcast.6, bf16[256,4096]{1,0:T(8,128)(2,1)} %bitcast.7, bf16[256,1024]{1,0:T(8,128)(2,1)} %bitcast.8, bf16[128,1024]{1,0:T(8,128)(2,1)} %w_own.1), custom_call_target="tpu_custom_call" | custom-call | tf_op jit(solution)/shard_map/pallas_call | solution.py:858
  52.7 3.2 %shard_map.77 = (bf16[256,4096]{1,0:T(8,128)(2,1)}, bf16[256,1024]{1,0:T(8,128)(2,1)}, bf16[256,4096]{1,0:T(8,128)(2,1)}) custom-call(bf16[256,4096]{1,0:T(8,128)(2,1)S(1)} %get-tuple-element.9.q_ref, bf16[256,1024]{1,0:T(8,128)(2,1)S(1)} %get-tuple-element.10.kv_ref, bf16[4096,1024]{1,0:T(8,128)(2,1)S(1)} %get-tuple-element.11.w_ref), custom_call_target="tpu_custom_call" | custom-call | tf_op jit(solution)/shard_map/pallas_call | solution.py:929
